TPU v7x, 512 devices: a whole 4x8x8 slice. The times are simulated.
512 devices in a mesh: wide: 32 (over z, x), narrow: 16 (over y, core).
Axes of the slice: x: 4, y: 8, z: 8, core: 2. Of those that a mesh axis runs over, the one named last changes fastest.
Arguments:
- excitation: bfloat16 [64, 2097152], P(None, ('wide', 'narrow')), may hold values from -6 to 6
- coords: bfloat16 [3, 2097152], P(None, ('wide', 'narrow')), may hold values from 0 to 1
- basis: bfloat16 [16, 2097152], P(None, ('wide', 'narrow')), may hold values from -0.5 to 0.5
- couplings: bfloat16 [262144, 256], P(('wide', 'narrow')), may hold values from -1.5 to 1.5
- near_list: int32 [16384, 24], P(('wide', 'narrow')), may hold values from 0 to 95
- far_dest: int32 [262144, 1], P(('wide', 'narrow')), may hold values from 0 to 511; in each aligned block of 512 rows (0 to 511, 512 to 1023, ...) at most 2 rows name the same one
- far_slot: int32 [262144], P(('wide', 'narrow')), may hold values from 0 to 31
- far_src: int32 [262144], P(('wide', 'narrow')), may hold values from 0 to 31
Outputs:
- potentials: bfloat16 [64, 2097152], P(None, ('wide', 'narrow'))
Inputs may be any that keep to these rules, and one draw needn't show every extreme that they name: `near_list`: k // 32 picks the previous (0), same (1) or next (2) device along narrow, k % 32 a cluster of it. `far_dest`: among the 512 pairs of one source device, at most 2 name the same receiving device; in some device's pairs one receiving device is named exactly 2 times.
All inputs are finite; a program needn't handle non-finite values.
Results may differ from a plain program's by a relative error of at most 0.0054.
Values may be sent and summed in bfloat16 or wider, within the bound.
A program may use at most 64 MiB of HBM per device.

v0:
```python
import functools
import math

import jax
import jax.numpy as jnp
from jax import lax
from jax.experimental import pallas as pl
from jax.experimental.pallas import tpu as pltpu
from jax.sharding import PartitionSpec as P

SOFTEN = 0.0025


def neighbours(value):
    devices = lax.axis_size("narrow")
    up = [(i, (i + 1) % devices) for i in range(devices - 1)]
    down = [(j, i) for i, j in up]
    return (lax.ppermute(value, "narrow", up), value, lax.ppermute(value, "narrow", down))


def split(value):
    high = value.astype(jnp.bfloat16).astype(jnp.float32)
    rest = value - high
    middle = rest.astype(jnp.bfloat16).astype(jnp.float32)
    return (high, middle, rest - middle)


def near_kernel(
    clusters, entries, panels, lists, field_before, field_own, field_after, coord_before, coord_own, coord_after,
    out, field, raw, sources, targets, sems,
):
    own = clusters * panels
    group = panels // 16
    copies = [
        pltpu.make_async_copy(part, field.at[:, pl.ds(i * own, own)], sems.at[i])
        for i, part in enumerate((field_before, field_own, field_after))
    ]
    for copy in copies:
        copy.start()
    raw[...] = jnp.zeros_like(raw)
    ones = jnp.ones((3, own), jnp.float32)
    lane_group = lax.broadcasted_iota(jnp.int32, (panels, panels), 1) // 16
    for i, part in enumerate((coord_before, coord_own, coord_after)):
        where = part[...].astype(jnp.float32)
        square = where[0:1] * where[0:1] + where[1:2] * where[1:2] + where[2:3] * where[2:3]
        if i == 1:
            raw[0:3, :] = where
            raw[6:9, :] = ones
            for row, value in enumerate(split(square + SOFTEN)):
                raw[3 + row : 4 + row, :] = value
            rows = raw[...].astype(jnp.bfloat16)
            for r in range(group):
                targets[16 * r : 16 * r + 16, :] = rows
        raw[0:3, :] = -2.0 * where
        raw[3:6, :] = ones
        for row, value in enumerate(split(square)):
            raw[6 + row : 7 + row, :] = value
        for g in range(clusters // group):
            block = jnp.concatenate(
                [raw[:, (group * g + r) * panels : (group * g + r + 1) * panels] for r in range(group)], axis=0
            ).T
            for r in range(group):
                start = (i * clusters + group * g + r) * panels
                sources[start : start + panels, :] = jnp.where(lane_group == r, block, 0.0).astype(jnp.bfloat16)
    for copy in copies:
        copy.wait()
    scale = 1.0 / math.sqrt(panels * entries)

    @pl.loop(0, clusters)
    def _(cluster):
        columns = pl.ds(pl.multiple_of(cluster * panels, panels), panels)
        target = targets[:, columns]
        total = jnp.zeros((out.shape[0], panels), jnp.float32)
        for entry in range(entries):
            source = pl.ds(pl.multiple_of(lists[cluster * entries + entry] * panels, panels), panels)
            distance = jnp.dot(sources[source, :], target, preferred_element_type=jnp.float32)
            kernel = lax.rsqrt(distance).astype(jnp.bfloat16)
            total += jnp.dot(field[:, source], kernel, preferred_element_type=jnp.float32)
        out[:, columns] = total * scale


def near_field(fields, coords, lists):
    clusters, entries = lists.shape
    columns_count, own = fields[1].shape
    panels = own // clusters
    whole = pl.BlockSpec(memory_space=pltpu.VMEM)
    anywhere = pl.BlockSpec(memory_space=pl.ANY)
    return pl.pallas_call(
        functools.partial(near_kernel, clusters, entries, panels),
        out_shape=jax.ShapeDtypeStruct((columns_count, own), jnp.float32),
        in_specs=[pl.BlockSpec(memory_space=pltpu.SMEM)] + [anywhere] * 3 + [whole] * 3,
        out_specs=whole,
        scratch_shapes=[
            pltpu.VMEM((columns_count, 3 * own), jnp.bfloat16),
            pltpu.VMEM((16, own), jnp.float32),
            pltpu.VMEM((3 * own, panels), jnp.bfloat16),
            pltpu.VMEM((panels, own), jnp.bfloat16),
            pltpu.SemaphoreType.DMA((3,)),
        ],
        compiler_params=pltpu.CompilerParams(vmem_limit_bytes=32 << 20),
        cost_estimate=pl.CostEstimate(flops=40_000_000_000, bytes_accessed=3_000_000, transcendentals=12_000_000),
    )(lists.reshape(-1), *fields, *coords)


def shards(excitation, coords, basis, couplings, near_list, far_dest, far_slot, far_src):
    columns_count, own_panels = excitation.shape
    clusters = near_list.shape[0]
    panels = own_panels // clusters
    basis_rank = basis.shape[0]
    pairs = far_src.shape[0]
    wide_count = lax.axis_size("wide")
    narrow_count = lax.axis_size("narrow")
    devices = wide_count * narrow_count
    capacity = max(2, 2 * pairs // devices)
    features = columns_count * basis_rank
    basis_blocks = basis.reshape(basis_rank, clusters, panels)
    coefficients = jnp.einsum(
        "ncp,rcp->cnr",
        excitation.reshape(columns_count, clusters, panels),
        basis_blocks,
        preferred_element_type=jnp.float32,
    ).astype(jnp.bfloat16)
    chosen = jnp.take(coefficients, far_src, axis=0)
    records = jnp.einsum(
        "pab,pnb->pna",
        couplings.reshape(pairs, basis_rank, basis_rank),
        chosen,
        preferred_element_type=jnp.float32,
    ).astype(jnp.bfloat16)
    records = records.reshape(pairs, features)
    destination = far_dest[:, 0]
    same_dest = destination[:, None] == destination[None, :]
    earlier = lax.broadcasted_iota(jnp.int32, (pairs, pairs), 1) < lax.broadcasted_iota(
        jnp.int32, (pairs, pairs), 0
    )
    order_within = jnp.sum((same_dest & earlier).astype(jnp.int32), axis=1)
    position = destination * capacity + order_within
    outgoing = jnp.zeros((devices * capacity, features), jnp.bfloat16).at[position].set(records)
    labels = jnp.full((devices * capacity,), -1, jnp.int32).at[position].set(far_slot)
    outgoing = outgoing.reshape(wide_count, narrow_count, capacity, features)
    labels = labels.reshape(wide_count, narrow_count, capacity)
    incoming, arrived = (
        lax.all_to_all(
            lax.all_to_all(outgoing, "wide", split_axis=0, concat_axis=0, tiled=True),
            "narrow",
            split_axis=1,
            concat_axis=1,
            tiled=True,
        ),
        lax.all_to_all(
            lax.all_to_all(labels, "wide", split_axis=0, concat_axis=0, tiled=True),
            "narrow",
            split_axis=1,
            concat_axis=1,
            tiled=True,
        ),
    )
    incoming = incoming.reshape(devices * capacity, features)
    arrived = arrived.reshape(devices * capacity)
    selector = (
        arrived[None, :] == lax.broadcasted_iota(jnp.int32, (clusters, devices * capacity), 0)
    ).astype(jnp.bfloat16)
    far_sums = jnp.dot(selector, incoming, preferred_element_type=jnp.float32)
    far_rounded = far_sums.astype(jnp.bfloat16).reshape(clusters, columns_count, basis_rank)
    far_field = jnp.einsum(
        "cnr,rcp->ncp", far_rounded, basis_blocks, preferred_element_type=jnp.float32
    ).reshape(columns_count, own_panels)
    near = near_field(neighbours(excitation), neighbours(coords), near_list)
    return (near + far_field).astype(jnp.bfloat16)


def solution(mesh):
    placed = (
        P(None, ("wide", "narrow")),
        P(None, ("wide", "narrow")),
        P(None, ("wide", "narrow")),
        P(("wide", "narrow"), None),
        P(("wide", "narrow"), None),
        P(("wide", "narrow"), None),
        P(("wide", "narrow")),
        P(("wide", "narrow")),
    )
    return jax.shard_map(
        shards, mesh=mesh, in_specs=placed, out_specs=P(None, ("wide", "narrow")), check_vma=False
    )
```

profile of v0, /device:TPU:1, one launch (start us, length us, event | category | flops | bytes accessed | tf_op | source)
XLA Modules:
  0.0 206.2 jit_solution(15643869869945297628)
XLA Ops:
  0.0 0.0 copy-start
  0.0 1.0 convert_reduce_fusion
  1.0 0.7 compare_select_fusion
  1.7 2.6 %scatter_custom_fusion = s32[1024]{0:T(1024)S(1)} fusion(s32[512]{0:T(512)S(1)} %bitcast.40, s32[512]{0:T(512)} %param.14, s32[]{:T(128)} %constant.8.clone.1), kind=kCustom, calls=%fused_computation.29 | custom fusion | bytes 4608 | tf_op jit(solution)/shard_map/scatter | solution.py:139
  4.3 0.2 reshape.39
  4.5 0.9 copy.79
  5.4 13.7 %all-to-all-start = ((s32[32,16,2]{1,2,0:T(2,128)}), s32[32,16,2]{1,2,0:T(2,128)S(1)}, u32[]{:S(2)}, u32[]{:S(2)}) async-start(s32[32,16,2]{1,2,0:T(2,128)} %copy.79), calls=%async_computation | async-start | bytes 65536 | tf_op jit(solution)/shard_map/all_to_all | solution.py:151
  19.1 0.7 compare_select_fusion.1
  19.8 0.7 compare_and_fusion
  20.5 1.1 copy.84
  21.6 2.8 %copy.85 = bf16[512,16,16]{2,1,0:T(8,128)(2,1)} copy(bf16[512,16,16]{0,2,1:T(8,128)(2,1)S(1)} %bitcast.37) | data formatting | bytes 524288 | tf_op jit(solution)/shard_map/reshape | solution.py:126
  24.4 0.0 copy-done
  24.4 0.4 convolution_convert_fusion
  24.8 2.1 gather_fusion
  26.9 4.2 %fusion.3 = bf16[512,64,16]{1,2,0:T(8,128)(2,1)} fusion(bf16[512,16,16]{2,1,0:T(8,128)(2,1)} %copy.85, bf16[512,64,16]{1,2,0:T(8,128)(2,1)S(1)} %gather_fusion, pred[512]{0:T(512)(128)(4,1)S(1)} %compare_and_fusion), kind=kOutput, calls=%fused_computation.6 | convolution fusion | flops 17825792 | bytes 2359808 | tf_op jit(solution)/shard_map/pab,pnb->pna/dot_general | solution.py:124
  31.0 3.5 %copy.86 = bf16[512,64,16]{0,2,1:T(8,128)(2,1)S(1)} copy(bf16[512,64,16]{1,2,0:T(8,128)(2,1)} %fusion.3) | data formatting | bytes 2097152 | tf_op jit(solution)/shard_map/convert_element_type | solution.py:129
  34.5 1.3 copy.87
  35.8 3.9 %scatter_custom_fusion.1 = bf16[1024,1024]{1,0:T(8,128)(2,1)S(1)} fusion(s32[512]{0:T(512)S(1)} %bitcast.41, bf16[512,1024]{1,0:T(8,128)(2,1)} %copy.87, bf16[]{:T(256)} %constant.6.clone.1), kind=kCustom, calls=%fused_computation.13 | custom fusion | bytes 2097664 | tf_op jit(solution)/shard_map/scatter | solution.py:138
  39.7 2.2 %reshape.44 = bf16[32,16,2,1024]{3,2,1,0:T(2,128)(2,1)} reshape(bf16[1024,1024]{1,0:T(8,128)(2,1)S(1)} %scatter_custom_fusion.1) | data formatting | bytes 4194304 | tf_op jit(solution)/shard_map/reshape | solution.py:140
  41.9 0.0 all-to-all-done
  41.9 9.3 %all-to-all-start.2 = ((bf16[32,16,2,1024]{3,2,1,0:T(2,128)(2,1)}), bf16[32,16,2,1024]{3,2,1,0:T(2,128)(2,1)}, u32[]{:S(2)}, u32[]{:S(2)}) async-start(bf16[32,16,2,1024]{3,2,1,0:T(2,128)(2,1)} %reshape.44), calls=%async_computation.2 | async-start | bytes 4194304 | tf_op jit(solution)/shard_map/all_to_all | solution.py:144
  51.3 4.6 %collective-permute-start = (bf16[64,4096]{1,0:T(8,128)(2,1)S(1)}, bf16[64,4096]{1,0:T(8,128)(2,1)S(1)}, u32[]{:S(2)}, u32[]{:S(2)}) collective-permute-start(bf16[64,4096]{1,0:T(8,128)(2,1)S(1)} %copy-done.1), channel_id=1, source_target_pairs={{0,1},{1,2},{2,3},{3,4},{4,5},{5,6},{6,7},{7,8},{8,9},{9,10},{10,1... | collective-permute-start | bytes 1572872 | tf_op jit(solution)/shard_map/ppermute | solution.py:18
  55.9 1.9 collective-permute-start.1
  57.8 0.7 copy.80
  58.5 40.7 %all-to-all-done.2 = bf16[32,16,2,1024]{3,2,1,0:T(2,128)(2,1)} async-done(((bf16[32,16,2,1024]{3,2,1,0:T(2,128)(2,1)}), bf16[32,16,2,1024]{3,2,1,0:T(2,128)(2,1)}, u32[]{:S(2)}, u32[]{:S(2)}) %all-to-all-start.2) | async-done | bytes 2097184 | tf_op jit(solution)/shard_map/all_to_all | solution.py:144
  99.2 10.3 %all-to-all-start.1 = ((s32[32,16,2]{0,2,1:T(2,128)}), s32[32,16,2]{0,2,1:T(2,128)S(1)}, u32[]{:S(2)}, u32[]{:S(2)}) async-start(s32[32,16,2]{0,2,1:T(2,128)} %copy.80), calls=%async_computation.1 | async-start | bytes 32768 | tf_op jit(solution)/shard_map/all_to_all | solution.py:150
  109.5 4.8 %copy.88 = bf16[32,16,2,1024]{3,2,0,1:T(2,128)(2,1)} copy(bf16[32,16,2,1024]{3,2,1,0:T(2,128)(2,1)} %all-to-all-done.2) | data formatting | bytes 4194304 | tf_op jit(solution)/shard_map/all_to_all | solution.py:144
  114.3 2.5 %all-to-all-done.1 = s32[32,16,2]{0,2,1:T(2,128)S(1)} async-done(((s32[32,16,2]{0,2,1:T(2,128)}), s32[32,16,2]{0,2,1:T(2,128)S(1)}, u32[]{:S(2)}, u32[]{:S(2)}) %all-to-all-start.1) | async-done | bytes 4128 | tf_op jit(solution)/shard_map/all_to_all | solution.py:150
  116.8 4.9 %all-to-all-start.3 = ((bf16[32,16,2,1024]{3,2,0,1:T(2,128)(2,1)}), bf16[32,16,2,1024]{3,2,0,1:T(2,128)(2,1)}, u32[]{:S(2)}, u32[]{:S(2)}) async-start(bf16[32,16,2,1024]{3,2,0,1:T(2,128)(2,1)} %copy.88), calls=%async_computation.3 | async-start | bytes 4194304 | tf_op jit(solution)/shard_map/all_to_all | solution.py:143
  121.7 3.5 %collective-permute-start.2 = (bf16[3,4096]{1,0:T(4,128)(2,1)S(1)}, bf16[3,4096]{1,0:T(4,128)(2,1)S(1)}, u32[]{:S(2)}, u32[]{:S(2)}) collective-permute-start(bf16[3,4096]{1,0:T(4,128)(2,1)S(1)} %copy-done.2), channel_id=1, source_target_pairs={{0,1},{1,2},{2,3},{3,4},{4,5},{5,6},{6,7},{7,8},{8,9},{9,10},{10,1... | collective-permute-start | bytes 73736 | tf_op jit(solution)/shard_map/ppermute | solution.py:18
  125.3 1.9 collective-permute-start.3
  127.2 0.1 copy.78
  127.3 0.1 reshape.38.lists
  127.4 0.2 copy.81
  127.6 0.2 eq.29
  127.7 39.9 %collective-permute-done.2.coord_before = bf16[3,4096]{1,0:T(4,128)(2,1)S(1)} collective-permute-done((bf16[3,4096]{1,0:T(4,128)(2,1)S(1)}, bf16[3,4096]{1,0:T(4,128)(2,1)S(1)}, u32[]{:S(2)}, u32[]{:S(2)}) %collective-permute-start.2) | collective-permute-done | bytes 24608 | tf_op jit(solution)/shard_map/ppermute | solution.py:18
  167.7 2.4 %collective-permute-done.3.coord_after = bf16[3,4096]{1,0:T(4,128)(2,1)S(1)} collective-permute-done((bf16[3,4096]{1,0:T(4,128)(2,1)S(1)}, bf16[3,4096]{1,0:T(4,128)(2,1)S(1)}, u32[]{:S(2)}, u32[]{:S(2)}) %collective-permute-start.3) | collective-permute-done | bytes 24608 | tf_op jit(solution)/shard_map/ppermute | solution.py:18
  170.1 0.0 collective-permute-done.field_before
  170.1 0.0 collective-permute-done.1.field_after
  170.1 23.1 %shard_map.82 = f32[64,4096]{1,0:T(8,128)S(1)} custom-call(s32[768]{0:T(1024)S(1)} %reshape.38.lists, bf16[64,4096]{1,0:T(8,128)(2,1)S(1)} %collective-permute-done.field_before, bf16[64,4096]{1,0:T(8,128)(2,1)S(1)} %copy-done.1, bf16[64,4096]{1,0:T(8,128)(2,1)S(1)} %collective-permute-done.1.field_after, ...), custom_call_target="tpu_custom_call" | custom-call | flops 40000000000 | bytes 3000000 | tf_op jit(solution)/shard_map/pallas_call | solution.py:88
  193.2 0.0 all-to-all-done.3
  193.2 5.1 %copy.89 = bf16[32,16,2,1024]{3,2,1,0:T(2,128)(2,1)} copy(bf16[32,16,2,1024]{3,2,0,1:T(2,128)(2,1)} %all-to-all-done.3) | data formatting | bytes 4194304 | tf_op jit(solution)/shard_map/all_to_all | solution.py:143
  198.3 4.1 %reshape.45 = bf16[1024,1024]{1,0:T(8,128)(2,1)} reshape(bf16[32,16,2,1024]{3,2,1,0:T(2,128)(2,1)} %copy.89) | data formatting | bytes 4194304 | tf_op jit(solution)/shard_map/reshape | solution.py:158
  202.4 2.0 convolution_convert_fusion.1
  204.4 0.2 copy.90
  204.6 0.3 copy.91
  204.9 0.3 convolution_bitcast_fusion
  205.3 0.9 fusion.6
  (7 shorter events, 0.0 us)
Async XLA Ops:
  0.0 24.4 %copy-start = (bf16[16,4096]{1,0:T(8,128)(2,1)S(1)}, bf16[16,4096]{1,0:T(8,128)(2,1)}, u32[]{:S(2)}) copy-start(bf16[16,4096]{1,0:T(8,128)(2,1)} %param.10) | copy-start | bytes 393220
  0.0 24.4 %copy-start.1 = (bf16[64,4096]{1,0:T(8,128)(2,1)S(1)}, bf16[64,4096]{1,0:T(8,128)(2,1)}, u32[]{:S(2)}) copy-start(bf16[64,4096]{1,0:T(8,128)(2,1)} %field_own.1) | copy-start | bytes 1572868
  5.4 36.6 %all-to-all-start = ((s32[32,16,2]{1,2,0:T(2,128)}), s32[32,16,2]{1,2,0:T(2,128)S(1)}, u32[]{:S(2)}, u32[]{:S(2)}) async-start(s32[32,16,2]{1,2,0:T(2,128)} %copy.79), calls=%async_computation | async-start | bytes 65536 | tf_op jit(solution)/shard_map/all_to_all | solution.py:151
  41.9 57.3 %all-to-all-start.2 = ((bf16[32,16,2,1024]{3,2,1,0:T(2,128)(2,1)}), bf16[32,16,2,1024]{3,2,1,0:T(2,128)(2,1)}, u32[]{:S(2)}, u32[]{:S(2)}) async-start(bf16[32,16,2,1024]{3,2,1,0:T(2,128)(2,1)} %reshape.44), calls=%async_computation.2 | async-start | bytes 4194304 | tf_op jit(solution)/shard_map/all_to_all | solution.py:144
  51.3 118.8 %collective-permute-start = (bf16[64,4096]{1,0:T(8,128)(2,1)S(1)}, bf16[64,4096]{1,0:T(8,128)(2,1)S(1)}, u32[]{:S(2)}, u32[]{:S(2)}) collective-permute-start(bf16[64,4096]{1,0:T(8,128)(2,1)S(1)} %copy-done.1), channel_id=1, source_target_pairs={{0,1},{1,2},{2,3},{3,4},{4,5},{5,6},{6,7},{7,8},{8,9},{9,10},{10,1... | collective-permute-start | bytes 1572872 | tf_op jit(solution)/shard_map/ppermute | solution.py:18
  55.9 114.2 %collective-permute-start.1 = (bf16[64,4096]{1,0:T(8,128)(2,1)S(1)}, bf16[64,4096]{1,0:T(8,128)(2,1)S(1)}, u32[]{:S(2)}, u32[]{:S(2)}) collective-permute-start(bf16[64,4096]{1,0:T(8,128)(2,1)S(1)} %copy-done.1), channel_id=1, source_target_pairs={{1,0},{2,1},{3,2},{4,3},{5,4},{6,5},{7,6},{8,7},{9,8},{10,9},{11,1... | collective-permute-start | bytes 1572872 | tf_op jit(solution)/shard_map/ppermute | solution.py:18
  99.2 17.6 %all-to-all-start.1 = ((s32[32,16,2]{0,2,1:T(2,128)}), s32[32,16,2]{0,2,1:T(2,128)S(1)}, u32[]{:S(2)}, u32[]{:S(2)}) async-start(s32[32,16,2]{0,2,1:T(2,128)} %copy.80), calls=%async_computation.1 | async-start | bytes 32768 | tf_op jit(solution)/shard_map/all_to_all | solution.py:150
  114.3 7.4 %copy-start.2 = (bf16[3,4096]{1,0:T(4,128)(2,1)S(1)}, bf16[3,4096]{1,0:T(4,128)(2,1)}, u32[]{:S(2)}) copy-start(bf16[3,4096]{1,0:T(4,128)(2,1)} %coord_own.1) | copy-start | bytes 73732
  114.3 12.9 %copy-start.3 = (s32[32,24]{0,1:T(8,128)S(1)}, s32[32,24]{0,1:T(8,128)}, u32[]{:S(2)}) copy-start(s32[32,24]{0,1:T(8,128)} %param.12) | copy-start | bytes 9220
  116.8 76.3 %all-to-all-start.3 = ((bf16[32,16,2,1024]{3,2,0,1:T(2,128)(2,1)}), bf16[32,16,2,1024]{3,2,0,1:T(2,128)(2,1)}, u32[]{:S(2)}, u32[]{:S(2)}) async-start(bf16[32,16,2,1024]{3,2,0,1:T(2,128)(2,1)} %copy.88), calls=%async_computation.3 | async-start | bytes 4194304 | tf_op jit(solution)/shard_map/all_to_all | solution.py:143
  121.7 45.9 %collective-permute-start.2 = (bf16[3,4096]{1,0:T(4,128)(2,1)S(1)}, bf16[3,4096]{1,0:T(4,128)(2,1)S(1)}, u32[]{:S(2)}, u32[]{:S(2)}) collective-permute-start(bf16[3,4096]{1,0:T(4,128)(2,1)S(1)} %copy-done.2), channel_id=1, source_target_pairs={{0,1},{1,2},{2,3},{3,4},{4,5},{5,6},{6,7},{7,8},{8,9},{9,10},{10,1... | collective-permute-start | bytes 73736 | tf_op jit(solution)/shard_map/ppermute | solution.py:18
  125.3 44.8 %collective-permute-start.3 = (bf16[3,4096]{1,0:T(4,128)(2,1)S(1)}, bf16[3,4096]{1,0:T(4,128)(2,1)S(1)}, u32[]{:S(2)}, u32[]{:S(2)}) collective-permute-start(bf16[3,4096]{1,0:T(4,128)(2,1)S(1)} %copy-done.2), channel_id=1, source_target_pairs={{1,0},{2,1},{3,2},{4,3},{5,4},{6,5},{7,6},{8,7},{9,8},{10,9},{11,1... | collective-permute-start | bytes 73736 | tf_op jit(solution)/shard_map/ppermute | solution.py:18
where the time goes:
time: 207 us; the launch traced here: 206 us
  waiting for transfers between devices  85.6 us (41%)
  starting transfers between devices  50.2 us (24%)
  local copies, waits for them, and re-layouts  36.3 us (18%)
  Pallas kernels  23.1 us (11%)
  matrix products  6.93 us (3%)
  other arithmetic  3.97 us (2%)
    all_to_all x1, waiting for transfers between devices, shards(): lax.all_to_all(outgoing, 'wide', split_axis=0, concat_axis=0, tiled=True)  40.7 us
    ppermute x2, waiting for transfers between devices, neighbours(): lax.ppermute(value, 'narrow', up)  39.9 us
    pallas_call x1, Pallas kernels, near_field(): pl.pallas_call(functools.partial(near_kernel, clusters, entries, panels),...  23.1 us
    all_to_all x1, starting transfers between devices, shards(): lax.all_to_all(labels, 'wide', split_axis=0, concat_axis=0, tiled=True)  13.7 us
    all_to_all x1, starting transfers between devices, shards(): lax.all_to_all(lax.all_to_all(labels, 'wide', split_axis=0, concat_axis=0...  10.3 us
    all_to_all x1, starting transfers between devices, shards(): lax.all_to_all(outgoing, 'wide', split_axis=0, concat_axis=0, tiled=True)  9.35 us
    ppermute x2, starting transfers between devices, neighbours(): lax.ppermute(value, 'narrow', up)  8.14 us
    all_to_all x1, local copies, waits for them, and re-layouts, shards(): lax.all_to_all(lax.all_to_all(outgoing, 'wide', split_axis=0, concat_axis...  5.09 us
  transfers between devices with their start and end apart: 8, of which 4 were waited for; matrix products, arithmetic and copies ran while one was open for 14% of the time, Pallas kernels for 11%

commit v1 on v0

v1 whole, which is shorter than its diff:
```python
import functools
import math

import jax
import jax.numpy as jnp
from jax import lax
from jax.experimental import pallas as pl
from jax.experimental.pallas import tpu as pltpu
from jax.sharding import PartitionSpec as P

SOFTEN = 0.0025
EARLY = 24
BF = jnp.bfloat16
F32 = jnp.float32
MESH = pl.DeviceIdType.MESH
NT = (((1,), (1,)), ((), ()))
WHOLE = pl.BlockSpec(memory_space=pltpu.VMEM)
ANYWHERE = pl.BlockSpec(memory_space=pl.ANY)


def onehot(condition):
    return jnp.where(condition, 1.0, 0.0).astype(BF)


def iota(shape, axis):
    return lax.broadcasted_iota(jnp.int32, shape, axis)


def split(value):
    high = value.astype(BF).astype(F32)
    rest = value - high
    middle = rest.astype(BF).astype(F32)
    return (high, middle, rest - middle)


def placement(sizes, dest, order):
    wide, narrow = sizes
    last = narrow // 2
    first = dest // (narrow * wide // last)
    across = (dest % narrow) // 2
    half_a = (dest % (narrow * wide // last), first * 2 + order, first)
    half_b = ((dest // narrow) * 2 + dest % 2, across * 2 + order, across)
    return (half_a, half_b)


def records_kernel(
    sizes, clusters, excitation, basis, couplings, dest, slot, source,
    send_a, send_b, label_a, label_b, blocks,
    coefficients, records,
):
    pairs, squared = couplings.shape
    rank = basis.shape[0]
    columns = excitation.shape[0]
    panels = excitation.shape[1] // clusters
    group = panels // rank
    for c in range(clusters):
        cut = slice(c * panels, (c + 1) * panels)
        blocks[c] = excitation[:, cut]
        coefficients[c * rank : (c + 1) * rank, :] = lax.dot_general(
            basis[:, cut], excitation[:, cut], NT, preferred_element_type=F32
        ).astype(BF)
    dest_down = jnp.broadcast_to(dest[...], (pairs, pairs))
    dest_along = jnp.broadcast_to(dest[...].astype(F32), (pairs, 128)).T[0:1].astype(jnp.int32)
    source_down = jnp.broadcast_to(source[...].astype(F32), (128, pairs)).T.astype(jnp.int32)
    same = (dest_down == dest_along) & (iota((pairs, pairs), 0) < iota((pairs, pairs), 1))
    order = jnp.sum(jnp.where(same, 1.0, 0.0), axis=0, keepdims=True).astype(jnp.int32)
    block = 128
    width = clusters * rank

    @pl.loop(0, rank // 2)
    def _(pair):
        lane = iota((squared, width), 1) % rank
        row = iota((squared, width), 0)
        spread = [onehot(row == (2 * pair + i) * rank + lane) for i in range(2)]
        for q in range(0, pairs, block):
            mine = jnp.concatenate([source_down[q : q + block]] * (width // 128), 1) == iota((block, width), 1) // rank
            parts = []
            for i in range(2):
                tiled = jnp.dot(couplings[q : q + block, :], spread[i], preferred_element_type=F32)
                chosen = jnp.where(mine, tiled, 0.0).astype(BF)
                parts.append(jnp.dot(chosen, coefficients[...], preferred_element_type=F32))
            records[q : q + block, pl.ds(pl.multiple_of(pair * 128, 128), 128)] = jnp.concatenate(parts, 1).astype(BF)

    half = records.shape[1] // 2
    for at, (partner, row, part), send, label in zip(
        (0, half), placement(sizes, dest_along, order), (send_a, send_b), (label_a, label_b)
    ):
        partners, rows = send.shape[0], send.shape[1]
        position = partner * rows + row
        for p in range(0, partners, 16):
            choice = onehot(position == iota((16 * rows, pairs), 0) + p * rows)
            packed = jnp.dot(choice, records[:, at : at + half], preferred_element_type=F32).astype(BF)
            send[p : p + 16] = packed.reshape(16, rows, half)
        code = (slot[...] + clusters * part + 1).astype(F32)
        left = jnp.where(partner == iota((partners, pairs), 0), code, 0.0).astype(BF)
        codes = lax.dot_general(left, onehot(row == iota((128, pairs), 0)), NT, preferred_element_type=F32)
        for p in range(partners):
            label[p] = codes[p : p + 1]


def outgoing(sizes, excitation, basis, couplings, far_dest, far_slot, far_src, clusters):
    columns, rank = excitation.shape[0], basis.shape[0]
    pairs = couplings.shape[0]
    wide, narrow = sizes
    last = narrow // 2
    partners = wide * narrow // last
    half = columns * rank // 2
    message = jax.ShapeDtypeStruct((partners, 2 * last, half), BF)
    codes = jax.ShapeDtypeStruct((partners, 1, 128), F32)
    blocks = jax.ShapeDtypeStruct((clusters, columns, excitation.shape[1] // clusters), BF)
    return pl.pallas_call(
        functools.partial(records_kernel, sizes, clusters),
        out_shape=(message, message, codes, codes, blocks),
        in_specs=[WHOLE] * 6,
        out_specs=(WHOLE,) * 5,
        scratch_shapes=[pltpu.VMEM((clusters * rank, columns), BF), pltpu.VMEM((pairs, 2 * half), BF)],
        compiler_params=pltpu.CompilerParams(vmem_limit_bytes=32 << 20),
    )(excitation, basis, couplings, far_dest, far_slot.reshape(1, pairs), far_src.reshape(1, pairs))


def main_kernel(
    sizes, clusters, entries, early,
    lists, coords, basis, send_a, send_b, label_a, label_b, excitation,
    out, field, coord_before, coord_after, raw, sources, targets, near,
    got_a, got_b, code_a, code_b, codes, part_a, part_b, sum_a, sum_b, spread,
    local_sem, halo_send, halo_recv, first_send, first_recv, last_send, last_recv,
):
    wide, narrow = sizes
    last = narrow // 2
    short = wide // last
    w, n = lax.axis_index("wide"), lax.axis_index("narrow")
    z, x, y, core = w // short, w % short, n // 2, n % 2
    columns, panels = excitation.shape[1:]
    own = clusters * panels
    rank = basis.shape[0]
    after, before = (n + 1) % narrow, (n + narrow - 1) % narrow

    halo = []
    for i, (source, target, device) in enumerate((
        (excitation, field.at[pl.ds(0, clusters)], after),
        (excitation, field.at[pl.ds(2 * clusters, clusters)], before),
        (coords, coord_before, after),
        (coords, coord_after, before),
    )):
        copy = pltpu.make_async_remote_copy(
            src_ref=source, dst_ref=target, send_sem=halo_send.at[i], recv_sem=halo_recv.at[i],
            device_id=(w, device), device_id_type=MESH,
        )
        copy.start()
        halo.append(copy)
    mine = pltpu.make_async_copy(excitation, field.at[pl.ds(clusters, clusters)], local_sem.at[0])
    mine.start()

    partners = send_a.shape[0]
    me_a, me_b = x * narrow + n, w * 2 + core

    def device_a(p):
        return (z * short + p // narrow, p % narrow)

    def device_b(p):
        return (p // 2, y * 2 + p % 2)

    groups = ((me_a, device_a, ((label_a, code_a), (send_a, got_a))), (me_b, device_b, ((label_b, code_b), (send_b, got_b))))

    @pl.loop(1, partners)
    def _(step):
        for g, (me, device, streams) in enumerate(groups):
            partner = (me + step) % partners
            for i, (send, got) in enumerate(streams):
                pltpu.make_async_remote_copy(
                    src_ref=send.at[partner], dst_ref=got.at[me],
                    send_sem=first_send.at[2 * g + i], recv_sem=first_recv.at[2 * g + i],
                    device_id=device(partner), device_id_type=MESH,
                ).start()

    for g, (me, device, streams) in enumerate(groups):
        for i, (send, got) in enumerate(streams):
            pltpu.make_async_copy(send.at[me], got.at[me], first_recv.at[2 * g + i]).start()

    group = panels // 16
    raw[...] = jnp.zeros_like(raw)
    ones = jnp.ones((3, own), F32)
    lane_group = iota((panels, panels), 1) // 16

    def prepare(i, part):
        where = part[...].astype(F32)
        square = where[0:1] * where[0:1] + where[1:2] * where[1:2] + where[2:3] * where[2:3]
        if i == 1:
            raw[0:3, :] = where
            raw[6:9, :] = ones
            for row, value in enumerate(split(square + SOFTEN)):
                raw[3 + row : 4 + row, :] = value
            rows = raw[...].astype(BF)
            for r in range(group):
                targets[16 * r : 16 * r + 16, :] = rows
        raw[0:3, :] = -2.0 * where
        raw[3:6, :] = ones
        for row, value in enumerate(split(square)):
            raw[6 + row : 7 + row, :] = value
        for g in range(clusters // group):
            block = jnp.concatenate(
                [raw[:, (group * g + r) * panels : (group * g + r + 1) * panels] for r in range(group)], axis=0
            ).T
            for r in range(group):
                sources[i * clusters + group * g + r] = jnp.where(lane_group == r, block, 0.0).astype(BF)

    prepare(1, coords)
    mine.wait()
    for copy in halo:
        copy.wait()
    prepare(0, coord_before)
    prepare(2, coord_after)

    @pl.when(n == 0)
    def _():
        field[0:clusters] = jnp.zeros((clusters, columns, panels), BF)

    @pl.when(n == narrow - 1)
    def _():
        field[2 * clusters : 3 * clusters] = jnp.zeros((clusters, columns, panels), BF)

    scale = 1.0 / math.sqrt(panels * entries)

    def near_clusters(start, stop):
        @pl.loop(start, stop)
        def _(cluster):
            cut = pl.ds(pl.multiple_of(cluster * panels, panels), panels)
            target = targets[:, cut]
            total = jnp.zeros((columns, panels), F32)
            for entry in range(entries):
                source = lists[cluster * entries + entry]
                distance = jnp.dot(sources[source], target, preferred_element_type=F32)
                kernel = lax.rsqrt(distance).astype(BF)
                total += jnp.dot(field[source], kernel, preferred_element_type=F32)
            near[:, cut] = total * scale

    near_clusters(0, early)

    rows = send_a.shape[1]
    half = send_a.shape[2]
    lasts = []
    for g, (got, code, part, final) in enumerate(((got_a, code_a, part_a, sum_a), (got_b, code_b, part_b, sum_b))):
        pltpu.make_async_copy(code, code, first_recv.at[2 * g]).wait()
        pltpu.make_async_copy(got, got, first_recv.at[2 * g + 1]).wait()
        for p in range(partners):
            codes[p : p + 1, :] = code[p]
        slots = partners * rows
        copied = jnp.dot(
            onehot(iota((slots, partners), 0) // rows == iota((slots, partners), 1)),
            codes[...].astype(BF),
            preferred_element_type=F32,
        )
        picked = jnp.where(iota((slots, 128), 0) % rows == iota((slots, 128), 1), copied, 0.0).astype(BF)
        along = lax.dot_general(jnp.ones((8, 128), BF), picked, NT, preferred_element_type=F32)[0:1].astype(jnp.int32)
        arrived = got[...].reshape(slots, half)
        for p in range(0, last, 2):
            choice = onehot(along == iota((2 * clusters, slots), 0) + (p * clusters + 1))
            sums = jnp.dot(choice, arrived, preferred_element_type=F32).astype(BF)
            part[p : p + 2] = sums.reshape(2, clusters, half)
        me = z if g == 0 else y

        @pl.loop(1, last)
        def _(step):
            there = (me + step) % last
            device = (there * short + x, n) if g == 0 else (w, there * 2 + core)
            pltpu.make_async_remote_copy(
                src_ref=part.at[there], dst_ref=final.at[me], send_sem=last_send.at[g], recv_sem=last_recv.at[g],
                device_id=device, device_id_type=MESH,
            ).start()

        pltpu.make_async_copy(part.at[me], final.at[me], last_recv.at[g]).start()

    near_clusters(early, clusters)

    count = rank // 2
    for g, final in enumerate((sum_a, sum_b)):
        pltpu.make_async_copy(final, final, last_recv.at[g]).wait()
        total = final[0].astype(F32)
        for p in range(1, last):
            total += final[p].astype(F32)
        total = total.astype(BF).astype(F32)
        for a in range(count):
            at = (g * count + a) * clusters
            spread[at : at + clusters, :] = total[:, a * columns : (a + 1) * columns]
    for c in range(clusters):
        cut = slice(c * panels, (c + 1) * panels)
        weights = spread[pl.ds(c, rank, stride=clusters), :].T.astype(BF)
        far = jnp.dot(weights, basis[:, cut], preferred_element_type=F32)
        out[:, cut] = (near[:, cut] + far).astype(BF)

    for g, (me, device, streams) in enumerate(groups):
        for i, (send, got) in enumerate(streams):
            most = pl.ds(0, partners - 1)
            pltpu.make_async_copy(send.at[most], send.at[most], first_send.at[2 * g + i]).wait()
    for g, part in enumerate((part_a, part_b)):
        most = pl.ds(0, last - 1)
        pltpu.make_async_copy(part.at[most], part.at[most], last_send.at[g]).wait()


def shards(excitation, coords, basis, couplings, near_list, far_dest, far_slot, far_src):
    columns, own = excitation.shape
    clusters, entries = near_list.shape
    panels = own // clusters
    rank = basis.shape[0]
    sizes = (lax.axis_size("wide"), lax.axis_size("narrow"))
    sent = outgoing(sizes, excitation, basis, couplings, far_dest, far_slot, far_src, clusters)
    partners, rows, half = sent[0].shape
    last = rows // 2
    dma = pltpu.SemaphoreType.DMA
    return pl.pallas_call(
        functools.partial(main_kernel, sizes, clusters, entries, EARLY),
        out_shape=jax.ShapeDtypeStruct((columns, own), BF),
        in_specs=[pl.BlockSpec(memory_space=pltpu.SMEM), WHOLE, WHOLE] + [ANYWHERE] * 5,
        out_specs=WHOLE,
        scratch_shapes=[
            pltpu.VMEM((3 * clusters, columns, panels), BF),
            pltpu.VMEM(coords.shape, BF),
            pltpu.VMEM(coords.shape, BF),
            pltpu.VMEM((16, own), F32),
            pltpu.VMEM((3 * clusters, panels, panels), BF),
            pltpu.VMEM((panels, own), BF),
            pltpu.VMEM((columns, own), F32),
        ]
        + [pltpu.VMEM((partners, rows, half), BF)] * 2
        + [pltpu.VMEM((partners, 1, 128), F32)] * 2
        + [pltpu.VMEM((partners, 128), F32)]
        + [pltpu.VMEM((last, clusters, half), BF)] * 4
        + [pltpu.VMEM((rank * clusters, columns), F32)]
        + [dma((1,)), dma((4,)), dma((4,)), dma((4,)), dma((4,)), dma((2,)), dma((2,))],
        compiler_params=pltpu.CompilerParams(vmem_limit_bytes=40 << 20, has_side_effects=True),
        cost_estimate=pl.CostEstimate(flops=40_000_000_000, bytes_accessed=6_000_000, transcendentals=12_000_000),
    )(near_list.reshape(-1), coords, basis, *sent)


def solution(mesh):
    placed = (
        P(None, ("wide", "narrow")),
        P(None, ("wide", "narrow")),
        P(None, ("wide", "narrow")),
        P(("wide", "narrow"), None),
        P(("wide", "narrow"), None),
        P(("wide", "narrow"), None),
        P(("wide", "narrow")),
        P(("wide", "narrow")),
    )
    return jax.shard_map(
        shards, mesh=mesh, in_specs=placed, out_specs=P(None, ("wide", "narrow")), check_vma=False
    )
```

time: 207 us -> 91.3 us (0.44)
  waiting for transfers between devices: 85.6 us -> 0 us
  Pallas kernels: 23.1 us -> 86.5 us
  starting transfers between devices: 50.2 us -> 0 us
  local copies, waits for them, and re-layouts: 36.3 us -> 4.49 us
  matrix products: 6.93 us -> 0 us
  other arithmetic: 3.97 us -> 0 us
    pallas_call x1 -> x2, Pallas kernels: 23.1 us -> 86.5 us  [the longest x1 71.9 us: shards(): pl.pallas_call(functools.partial(main_kernel, sizes, clusters, entries, E...]
    all_to_all x4 -> x0, waiting for transfers between devices: 43.2 us -> none  [the longest x1 40.7 us: shards(): lax.all_to_all(outgoing, 'wide', split_axis=0, concat_axis=0, tiled=True)]
    ppermute x4 -> x0, waiting for transfers between devices: 42.3 us -> none  [the longest x2 39.9 us: neighbours(): lax.ppermute(value, 'narrow', up)]
    all_to_all x4 -> x0, starting transfers between devices: 38.2 us -> none  [the longest x1 13.7 us: shards(): lax.all_to_all(labels, 'wide', split_axis=0, concat_axis=0, tiled=True)]
    ppermute x4 -> x0, starting transfers between devices: 12 us -> none  [the longest x2 8.14 us: neighbours(): lax.ppermute(value, 'narrow', up)]
    reshape x8 -> x1, local copies, waits for them, and re-layouts: 11.9 us -> 0.08 us  [shards(): near_list.reshape(-1)]
    all_to_all x4 -> x0, local copies, waits for them, and re-layouts: 10.8 us -> none  [the longest x1 5.09 us: shards(): lax.all_to_all(lax.all_to_all(outgoing, 'wide', split_axis=0, concat_axis...]
    dot_general x4 -> x0, matrix products: 6.93 us -> none  [the longest x1 4.19 us: shards(): jnp.einsum('pab,pnb->pna', couplings.reshape(pairs, basis_rank, basis_ran...]
  transfers between devices with their start and end apart: 8 -> 0, of which waited for: 4 -> 0; matrix products, arithmetic and copies ran while one was open for 14% -> 0% of each run, Pallas kernels for 11% -> 0%
where the time goes in v1:
time: 91.3 us; the launch traced here: 91.1 us
  Pallas kernels  86.5 us (95%)
  local copies, waits for them, and re-layouts  4.49 us (5%)
    pallas_call x1, Pallas kernels, shards(): pl.pallas_call(functools.partial(main_kernel, sizes, clusters, entries, E...  71.9 us
    pallas_call x1, Pallas kernels, outgoing(): pl.pallas_call(functools.partial(records_kernel, sizes, clusters), out_sh...  14.7 us
    unnamed x17, local copies, waits for them, and re-layouts  4.41 us

profile of v1, /device:TPU:1, one launch (start us, length us, event | category | flops | bytes accessed | tf_op | source)
XLA Modules:
  0.0 91.1 jit_solution(17578279944151971942)
XLA Ops:
  0.0 0.0 copy-start.1
  0.0 0.8 copy.10
  0.8 0.1 reshape.9.lists
  0.9 0.0 copy-start.4
  0.9 0.0 copy-start.5
  0.9 0.8 copy.11.dest
  1.8 0.0 copy-done.1
  1.8 0.0 copy-done.4
  1.8 0.0 copy-done.5
  1.8 0.0 copy-start
  1.8 1.0 %copy-done = bf16[64,4096]{1,0:T(8,128)(2,1)S(1)} copy-done((bf16[64,4096]{1,0:T(8,128)(2,1)S(1)}, bf16[64,4096]{1,0:T(8,128)(2,1)}, u32[]{:S(2)}) %copy-start) | copy-done | bytes 524312
  2.9 0.0 copy-start.2
  2.9 0.9 copy-done.2
  3.8 0.0 copy-start.3
  3.8 0.0 copy-start.6
  3.8 14.7 %shard_map.82 = (bf16[64,16,512]{2,1,0:T(8,128)(2,1)S(1)}, bf16[64,16,512]{2,1,0:T(8,128)(2,1)S(1)}, f32[64,1,128]{2,1,0:T(1,128)S(1)}, f32[64,1,128]{2,1,0:T(1,128)S(1)}, bf16[32,64,128]{2,1,0:T(8,128)(2,1)S(1)}) custom-call(bf16[64,4096]{1,0:T(8,128)(2,1)S(1)} %copy-done, bf16[16,4096]{1,0:T(8,128)(2,1)S(1)} %copy-done.2, bf16[512,256]{1,0:T(8,128)(2,1)S(1)} %copy-done.1, ...), custom_call_target="tpu_custom_call" | custom-call | tf_op jit(solution)/shard_map/pallas_call | solution.py:111
  18.4 0.0 copy-done.3
  18.4 0.0 copy-done.6
  18.4 71.9 %shard_map.83 = bf16[64,4096]{1,0:T(8,128)(2,1)S(1)} custom-call(s32[768]{0:T(1024)S(1)} %reshape.9.lists, bf16[3,4096]{1,0:T(4,128)(2,1)S(1)} %copy-done.6, bf16[16,4096]{1,0:T(8,128)(2,1)S(1)} %copy-done.3, bf16[64,16,512]{2,1,0:T(8,128)(2,1)S(1)} %get-tuple-element.10.send_a, bf16[64,16,512]{2,1,0:T(8,128)(2,1)S(1)} %get-tuple-element.11.send_b, ...), custom_call_target="tpu_custom_call" | custom-call | flops 40000000000 | bytes 6000000 | tf_op jit(solution)/shard_map/pallas_call | solution.py:310
  90.3 0.8 copy.13
Async XLA Ops:
  0.0 1.8 %copy-start.1 = (bf16[512,256]{1,0:T(8,128)(2,1)S(1)}, bf16[512,256]{1,0:T(8,128)(2,1)}, u32[]{:S(2)}) copy-start(bf16[512,256]{1,0:T(8,128)(2,1)} %couplings.1) | copy-start | bytes 786436
  0.9 0.9 copy-start.4
  0.9 0.9 copy-start.5
  1.8 1.0 %copy-start = (bf16[64,4096]{1,0:T(8,128)(2,1)S(1)}, bf16[64,4096]{1,0:T(8,128)(2,1)}, u32[]{:S(2)}) copy-start(bf16[64,4096]{1,0:T(8,128)(2,1)} %excitation.1) | copy-start | bytes 1572868
  2.9 0.9 copy-start.2
  3.8 14.7 %copy-start.3 = (bf16[16,4096]{1,0:T(8,128)(2,1)S(1)}, bf16[16,4096]{1,0:T(8,128)(2,1)}, u32[]{:S(2)}) copy-start(bf16[16,4096]{1,0:T(8,128)(2,1)} %basis.3) | copy-start | bytes 393220
  3.8 14.7 %copy-start.6 = (bf16[3,4096]{1,0:T(4,128)(2,1)S(1)}, bf16[3,4096]{1,0:T(4,128)(2,1)}, u32[]{:S(2)}) copy-start(bf16[3,4096]{1,0:T(4,128)(2,1)} %coords.1) | copy-start | bytes 73732

commit v2 on v1

v2 whole, which is shorter than its diff:
```python
import functools
import math

import jax
import jax.numpy as jnp
from jax import lax
from jax.experimental import pallas as pl
from jax.experimental.pallas import tpu as pltpu
from jax.sharding import PartitionSpec as P

SOFTEN = 0.0025
FIRST_NEAR = 20
SECOND_NEAR = 25
BF = jnp.bfloat16
F32 = jnp.float32
MESH = pl.DeviceIdType.MESH
NT = (((1,), (1,)), ((), ()))
WHOLE = pl.BlockSpec(memory_space=pltpu.VMEM)
ANYWHERE = pl.BlockSpec(memory_space=pltpu.HBM)


def onehot(condition):
    return jnp.where(condition, 1.0, 0.0).astype(BF)


def iota(shape, axis):
    return lax.broadcasted_iota(jnp.int32, shape, axis)


def split(value):
    high = value.astype(BF).astype(F32)
    rest = value - high
    middle = rest.astype(BF).astype(F32)
    return (high, middle, rest - middle)


def placement(sizes, dest, order):
    wide, narrow = sizes
    last = narrow // 2
    first = dest // (narrow * wide // last)
    across = (dest % narrow) // 2
    half_a = (dest % (narrow * wide // last), first * 2 + order, first)
    half_b = ((dest // narrow) * 2 + dest % 2, across * 2 + order, across)
    return (half_a, half_b)


def main_kernel(
    sizes, clusters, entries,
    lists, excitation, coords, basis, couplings, dest, slot, origin,
    out, field, coord_before, coord_after, raw, sources, targets, near,
    own_field, own_coords, own_basis, own_couplings, source_down, coefficients, records,
    send_a, send_b, label_a, label_b,
    got_a, got_b, code_a, code_b, codes, part_a, part_b, sum_a, sum_b, spread,
    local_sem, halo_send, halo_recv, first_send, first_recv, last_send, last_recv,
):
    wide, narrow = sizes
    last = narrow // 2
    short = wide // last
    w, n = lax.axis_index("wide"), lax.axis_index("narrow")
    z, x, y, core = w // short, w % short, n // 2, n % 2
    columns, own = excitation.shape
    panels = own // clusters
    rank = basis.shape[0]
    pairs = couplings.shape[0]
    group = panels // rank
    partners, rows, half = send_a.shape
    after, before = (n + 1) % narrow, (n + narrow - 1) % narrow
    me_a, me_b = x * narrow + n, w * 2 + core

    def device_a(p):
        return (z * short + p // narrow, p % narrow)

    def device_b(p):
        return (p // 2, y * 2 + p % 2)

    groups = ((me_a, device_a, ((label_a, code_a), (send_a, got_a))), (me_b, device_b, ((label_b, code_b), (send_b, got_b))))

    barrier = pltpu.get_barrier_semaphore()

    @pl.loop(1, partners)
    def _(step):
        for me, device, _ in groups:
            pl.semaphore_signal(barrier, inc=1, device_id=device((me + step) % partners), device_id_type=MESH)

    loads = [
        pltpu.make_async_copy(source, target, local_sem.at[i])
        for i, (source, target) in enumerate(
            ((excitation, own_field), (basis, own_basis), (couplings, own_couplings), (coords, own_coords))
        )
    ]
    for load in loads:
        load.start()

    dest_along = dest[...]
    dest_down = jnp.broadcast_to(dest_along.astype(F32), (128, pairs)).T
    source_down[...] = jnp.broadcast_to(origin[...].astype(F32), (128, pairs)).T
    orders = []
    for p in range(0, pairs, 128):
        same = (dest_down == dest_along[:, p : p + 128].astype(F32)) & (iota((pairs, 128), 0) < iota((pairs, 128), 1) + p)
        orders.append(jnp.sum(jnp.where(same, 1.0, 0.0), axis=0, keepdims=True))
    order = jnp.concatenate(orders, 1).astype(jnp.int32)
    places = placement(sizes, dest_along, order)

    loads[0].wait()
    for c in range(clusters):
        field[clusters + c] = own_field[:, c * panels : (c + 1) * panels]
    for load in loads[1:]:
        load.wait()
    for c in range(clusters):
        coefficients[c * rank : (c + 1) * rank, :] = lax.dot_general(
            own_basis[:, c * panels : (c + 1) * panels], field[clusters + c], NT, preferred_element_type=F32
        ).astype(BF)

    pl.semaphore_wait(barrier, 2 * (partners - 1))

    halo = []
    middle = field.at[pl.ds(clusters, clusters)]
    for i, (source, target, device) in enumerate((
        (middle, field.at[pl.ds(0, clusters)], after),
        (middle, field.at[pl.ds(2 * clusters, clusters)], before),
        (own_coords, coord_before, after),
        (own_coords, coord_after, before),
    )):
        copy = pltpu.make_async_remote_copy(
            src_ref=source, dst_ref=target, send_sem=halo_send.at[i], recv_sem=halo_recv.at[i],
            device_id=(w, device), device_id_type=MESH,
        )
        copy.start()
        halo.append(copy)

    block = 64
    lane = iota((block, 128), 1)
    for q in range(0, pairs, block):
        at = slice(q, q + block)
        mine = [source_down[at, :] == (lane // rank + g * group).astype(F32) for g in range(clusters // group)]
        for pair in range(rank // 2):
            products = []
            for a in (2 * pair, 2 * pair + 1):
                across = own_couplings[at, (a // group) * 128 : (a // group + 1) * 128].astype(F32)
                tiled = jnp.take_along_axis(across, (a % group) * rank + lane % rank, axis=1)
                chosen = jnp.concatenate([jnp.where(m, tiled, 0.0).astype(BF) for m in mine], 1)
                products.append(jnp.dot(chosen, coefficients[...], preferred_element_type=F32))
            records[at, pair * 128 : (pair + 1) * 128] = jnp.concatenate(products, 1).astype(BF)

    for g, ((partner, row, part), (me, device, streams)) in enumerate(zip(places, groups)):
        (label, code), (send, got) = streams
        position = partner * rows + row
        for p in range(0, partners, 16):
            choice = onehot(position == iota((16 * rows, pairs), 0) + p * rows)
            packed = jnp.dot(choice, records[:, g * half : (g + 1) * half], preferred_element_type=F32).astype(BF)
            send[p : p + 16] = packed.reshape(16, rows, half)
        numbers = (slot[...] + clusters * part + 1).astype(F32)
        left = jnp.where(partner == iota((partners, pairs), 0), numbers, 0.0).astype(BF)
        table = lax.dot_general(left, onehot(row == iota((128, pairs), 0)), NT, preferred_element_type=F32)
        for p in range(partners):
            label[p] = table[p : p + 1]

        @pl.loop(1, partners)
        def _(step):
            there = (me + step) % partners
            for i, (source, target) in enumerate(streams):
                pltpu.make_async_remote_copy(
                    src_ref=source.at[there], dst_ref=target.at[me],
                    send_sem=first_send.at[2 * g + i], recv_sem=first_recv.at[2 * g + i],
                    device_id=device(there), device_id_type=MESH,
                ).start()

        for i, (source, target) in enumerate(streams):
            pltpu.make_async_copy(source.at[me], target.at[me], first_recv.at[2 * g + i]).start()

    raw[...] = jnp.zeros_like(raw)
    ones = jnp.ones((3, own), F32)
    lane_group = iota((panels, panels), 1) // 16

    def prepare(i, part):
        where = part[...].astype(F32)
        square = where[0:1] * where[0:1] + where[1:2] * where[1:2] + where[2:3] * where[2:3]
        if i == 1:
            raw[0:3, :] = where
            raw[6:9, :] = ones
            for row, value in enumerate(split(square + SOFTEN)):
                raw[3 + row : 4 + row, :] = value
            rows = raw[...].astype(BF)
            for r in range(group):
                targets[16 * r : 16 * r + 16, :] = rows
        raw[0:3, :] = -2.0 * where
        raw[3:6, :] = ones
        for row, value in enumerate(split(square)):
            raw[6 + row : 7 + row, :] = value
        for g in range(clusters // group):
            block = jnp.concatenate(
                [raw[:, (group * g + r) * panels : (group * g + r + 1) * panels] for r in range(group)], axis=0
            ).T
            for r in range(group):
                sources[i * clusters + group * g + r] = jnp.where(lane_group == r, block, 0.0).astype(BF)

    prepare(1, own_coords)
    for copy in halo:
        copy.wait()
    prepare(0, coord_before)
    prepare(2, coord_after)

    @pl.when(n == 0)
    def _():
        field[0:clusters] = jnp.zeros((clusters, columns, panels), BF)

    @pl.when(n == narrow - 1)
    def _():
        field[2 * clusters : 3 * clusters] = jnp.zeros((clusters, columns, panels), BF)

    scale = 1.0 / math.sqrt(panels * entries)

    def near_clusters(start, stop):
        @pl.loop(start, stop)
        def _(cluster):
            cut = pl.ds(pl.multiple_of(cluster * panels, panels), panels)
            target = targets[:, cut]
            total = jnp.zeros((columns, panels), F32)
            for entry in range(entries):
                source = lists[entry, cluster]
                distance = jnp.dot(sources[source], target, preferred_element_type=F32)
                kernel = lax.rsqrt(distance).astype(BF)
                total += jnp.dot(field[source], kernel, preferred_element_type=F32)
            near[:, cut] = total * scale

    for g, (got, code, part, final) in enumerate(((got_a, code_a, part_a, sum_a), (got_b, code_b, part_b, sum_b))):
        near_clusters(0 if g == 0 else FIRST_NEAR, FIRST_NEAR if g == 0 else SECOND_NEAR)
        pltpu.make_async_copy(code, code, first_recv.at[2 * g]).wait()
        pltpu.make_async_copy(got, got, first_recv.at[2 * g + 1]).wait()
        for p in range(partners):
            codes[p : p + 1, :] = code[p]
        slots = partners * rows
        copied = jnp.dot(
            onehot(iota((slots, partners), 0) // rows == iota((slots, partners), 1)),
            codes[...].astype(BF),
            preferred_element_type=F32,
        )
        picked = jnp.where(iota((slots, 128), 0) % rows == iota((slots, 128), 1), copied, 0.0).astype(BF)
        along = lax.dot_general(jnp.ones((8, 128), BF), picked, NT, preferred_element_type=F32)[0:1].astype(jnp.int32)
        arrived = got[...].reshape(slots, half)
        for p in range(0, last, 2):
            choice = onehot(along == iota((2 * clusters, slots), 0) + (p * clusters + 1))
            sums = jnp.dot(choice, arrived, preferred_element_type=F32).astype(BF)
            part[p : p + 2] = sums.reshape(2, clusters, half)
        me = z if g == 0 else y

        @pl.loop(1, last)
        def _(step):
            there = (me + step) % last
            device = (there * short + x, n) if g == 0 else (w, there * 2 + core)
            pltpu.make_async_remote_copy(
                src_ref=part.at[there], dst_ref=final.at[me], send_sem=last_send.at[g], recv_sem=last_recv.at[g],
                device_id=device, device_id_type=MESH,
            ).start()

        pltpu.make_async_copy(part.at[me], final.at[me], last_recv.at[g]).start()

    near_clusters(SECOND_NEAR, clusters)

    count = rank // 2
    for g, final in enumerate((sum_a, sum_b)):
        pltpu.make_async_copy(final, final, last_recv.at[g]).wait()
        total = final[0].astype(F32)
        for p in range(1, last):
            total += final[p].astype(F32)
        total = total.astype(BF).astype(F32)
        for a in range(count):
            at = (g * count + a) * clusters
            spread[at : at + clusters, :] = total[:, a * columns : (a + 1) * columns]
    for c in range(clusters):
        cut = slice(c * panels, (c + 1) * panels)
        weights = spread[pl.ds(c, rank, stride=clusters), :].T.astype(BF)
        far = jnp.dot(weights, own_basis[:, cut], preferred_element_type=F32)
        out[:, cut] = (near[:, cut] + far).astype(BF)

    for g, (me, device, streams) in enumerate(groups):
        for i, (send, got) in enumerate(streams):
            most = pl.ds(0, partners - 1)
            pltpu.make_async_copy(send.at[most], send.at[most], first_send.at[2 * g + i]).wait()
    for g, part in enumerate((part_a, part_b)):
        most = pl.ds(0, last - 1)
        pltpu.make_async_copy(part.at[most], part.at[most], last_send.at[g]).wait()


def shards(excitation, coords, basis, couplings, near_list, far_dest, far_slot, far_src):
    columns, own = excitation.shape
    clusters, entries = near_list.shape
    panels = own // clusters
    rank = basis.shape[0]
    pairs, squared = couplings.shape
    wide, narrow = lax.axis_size("wide"), lax.axis_size("narrow")
    last = narrow // 2
    partners, rows, half = wide * narrow // last, 2 * last, columns * rank // 2
    dma = pltpu.SemaphoreType.DMA
    return pl.pallas_call(
        functools.partial(main_kernel, (wide, narrow), clusters, entries),
        out_shape=jax.ShapeDtypeStruct((columns, own), BF),
        in_specs=[pl.BlockSpec(memory_space=pltpu.SMEM)] + [ANYWHERE] * 4 + [WHOLE] * 3,
        out_specs=WHOLE,
        scratch_shapes=[
            pltpu.VMEM((3 * clusters, columns, panels), BF),
            pltpu.VMEM(coords.shape, BF),
            pltpu.VMEM(coords.shape, BF),
            pltpu.VMEM((16, own), F32),
            pltpu.VMEM((3 * clusters, panels, panels), BF),
            pltpu.VMEM((panels, own), BF),
            pltpu.VMEM((columns, own), F32),
            pltpu.VMEM(excitation.shape, BF),
            pltpu.VMEM(coords.shape, BF),
            pltpu.VMEM(basis.shape, BF),
            pltpu.VMEM(couplings.shape, BF),
            pltpu.VMEM((pairs, 128), F32),
            pltpu.VMEM((clusters * rank, columns), BF),
            pltpu.VMEM((pairs, 2 * half), BF),
        ]
        + [pltpu.VMEM((partners, rows, half), BF)] * 2
        + [pltpu.VMEM((partners, 1, 128), F32)] * 2
        + [pltpu.VMEM((partners, rows, half), BF)] * 2
        + [pltpu.VMEM((partners, 1, 128), F32)] * 2
        + [pltpu.VMEM((partners, 128), F32)]
        + [pltpu.VMEM((last, clusters, half), BF)] * 4
        + [pltpu.VMEM((rank * clusters, columns), F32)]
        + [dma((4,)), dma((4,)), dma((4,)), dma((4,)), dma((4,)), dma((2,)), dma((2,))],
        compiler_params=pltpu.CompilerParams(vmem_limit_bytes=48 << 20, has_side_effects=True, collective_id=0),
        cost_estimate=pl.CostEstimate(flops=40_000_000_000, bytes_accessed=6_000_000, transcendentals=12_000_000),
    )(
        near_list.T, excitation, coords, basis, couplings,
        far_dest.reshape(1, pairs), far_slot.reshape(1, pairs), far_src.reshape(1, pairs),
    )


def solution(mesh):
    placed = (
        P(None, ("wide", "narrow")),
        P(None, ("wide", "narrow")),
        P(None, ("wide", "narrow")),
        P(("wide", "narrow"), None),
        P(("wide", "narrow"), None),
        P(("wide", "narrow"), None),
        P(("wide", "narrow")),
        P(("wide", "narrow")),
    )
    return jax.shard_map(
        shards, mesh=mesh, in_specs=placed, out_specs=P(None, ("wide", "narrow")), check_vma=False
    )
```

time: 91.3 us -> 71.5 us (0.78)
  Pallas kernels: 86.5 us -> 64.9 us
  local copies, waits for them, and re-layouts: 4.49 us -> 5.86 us
    pallas_call x2 -> x1, Pallas kernels: 86.5 us -> 64.9 us  [shards(): pl.pallas_call(functools.partial(main_kernel, (wide, narrow), clusters, e...]
    unnamed x17, local copies, waits for them, and re-layouts: 4.41 us -> 5.86 us
where the time goes in v2:
time: 71.5 us; the launch traced here: 70.8 us
  Pallas kernels  64.9 us (91%)
  local copies, waits for them, and re-layouts  5.86 us (8%)
    pallas_call x1, Pallas kernels, shards(): pl.pallas_call(functools.partial(main_kernel, (wide, narrow), clusters, e...  64.9 us
    unnamed x17, local copies, waits for them, and re-layouts  5.86 us

profile of v2, /device:TPU:1, one launch (start us, length us, event | category | flops | bytes accessed | tf_op | source)
XLA Modules:
  0.0 70.8 jit_solution(17066984020528819591)
XLA Ops:
  0.0 0.0 copy-start.7
  0.0 0.0 copy-start.6
  0.0 0.0 copy-start.5
  0.0 0.7 copy-done.7
  0.7 0.0 copy-done.6
  0.7 0.0 copy-done.5
  0.7 0.0 copy-start
  0.7 1.0 %copy-done = bf16[64,4096]{1,0:T(8,128)(2,1)S(1)} copy-done((bf16[64,4096]{1,0:T(8,128)(2,1)S(1)}, bf16[64,4096]{1,0:T(8,128)(2,1)}, u32[]{:S(2)}) %copy-start) | copy-done | bytes 524312
  1.8 0.0 copy-start.1
  1.8 0.9 %copy-done.1 = bf16[512,256]{1,0:T(8,128)(2,1)S(1)} copy-done((bf16[512,256]{1,0:T(8,128)(2,1)S(1)}, bf16[512,256]{1,0:T(8,128)(2,1)}, u32[]{:S(2)}) %copy-start.1) | copy-done | bytes 262168
  2.7 0.0 copy-start.2
  2.7 0.9 %copy-done.2 = bf16[16,4096]{1,0:T(8,128)(2,1)S(1)} copy-done((bf16[16,4096]{1,0:T(8,128)(2,1)S(1)}, bf16[16,4096]{1,0:T(8,128)(2,1)}, u32[]{:S(2)}) %copy-start.2) | copy-done | bytes 131096
  3.6 0.0 copy-start.3
  3.6 0.8 %copy-done.3 = bf16[3,4096]{1,0:T(4,128)(2,1)S(1)} copy-done((bf16[3,4096]{1,0:T(4,128)(2,1)S(1)}, bf16[3,4096]{1,0:T(4,128)(2,1)}, u32[]{:S(2)}) %copy-start.3) | copy-done | bytes 24600
  4.4 0.0 copy-start.4
  4.4 0.7 copy-done.4
  5.1 64.9 %shard_map.82 = bf16[64,4096]{1,0:T(8,128)(2,1)S(1)} custom-call(s32[24,32]{1,0:T(8,128)S(1)} %bitcast.4, bf16[64,4096]{1,0:T(8,128)(2,1)S(1)} %copy-done, bf16[3,4096]{1,0:T(4,128)(2,1)S(1)} %copy-done.3, bf16[16,4096]{1,0:T(8,128)(2,1)S(1)} %copy-done.2, bf16[512,256]{1,0:T(8,128)(2,1)S(1)} %copy-done.1, s32[1,512]{1,0:T(1,128)S(1)} %bitcast.5, ...), custom_call_target="tpu_custom_call" | custom-call | flops 40000000000 | bytes 6000000 | tf_op jit(solution)/shard_map/pallas_call | solution.py:295
  70.0 0.8 %copy.10 = bf16[64,4096]{1,0:T(8,128)(2,1)} copy(bf16[64,4096]{1,0:T(8,128)(2,1)S(1)} %shard_map.82) | data formatting | bytes 1048576
Async XLA Ops:
  0.0 0.7 copy-start.7
  0.0 0.7 copy-start.6
  0.0 0.7 %copy-start.5 = (s32[512,1]{0,1:T(1,128)S(1)}, s32[512,1]{0,1:T(1,128)}, u32[]{:S(2)}) copy-start(s32[512,1]{0,1:T(1,128)} %param.13) | copy-start | bytes 6148
  0.7 1.0 %copy-start = (bf16[64,4096]{1,0:T(8,128)(2,1)S(1)}, bf16[64,4096]{1,0:T(8,128)(2,1)}, u32[]{:S(2)}) copy-start(bf16[64,4096]{1,0:T(8,128)(2,1)} %excitation.1) | copy-start | bytes 1572868
  1.8 0.9 %copy-start.1 = (bf16[512,256]{1,0:T(8,128)(2,1)S(1)}, bf16[512,256]{1,0:T(8,128)(2,1)}, u32[]{:S(2)}) copy-start(bf16[512,256]{1,0:T(8,128)(2,1)} %couplings.1) | copy-start | bytes 786436
  2.7 0.9 %copy-start.2 = (bf16[16,4096]{1,0:T(8,128)(2,1)S(1)}, bf16[16,4096]{1,0:T(8,128)(2,1)}, u32[]{:S(2)}) copy-start(bf16[16,4096]{1,0:T(8,128)(2,1)} %basis.1) | copy-start | bytes 393220
  3.6 0.8 %copy-start.3 = (bf16[3,4096]{1,0:T(4,128)(2,1)S(1)}, bf16[3,4096]{1,0:T(4,128)(2,1)}, u32[]{:S(2)}) copy-start(bf16[3,4096]{1,0:T(4,128)(2,1)} %coords.1) | copy-start | bytes 73732
  4.4 0.7 copy-start.4

commit v3 on v2

--- a/solution.py
+++ b/solution.py
@@ -9,8 +9,8 @@
 from jax.sharding import PartitionSpec as P
 
 SOFTEN = 0.0025
-FIRST_NEAR = 20
-SECOND_NEAR = 25
+FIRST_NEAR = 18
+SECOND_NEAR = 20
 BF = jnp.bfloat16
 F32 = jnp.float32
 MESH = pl.DeviceIdType.MESH
@@ -51,7 +51,7 @@
     own_field, own_coords, own_basis, own_couplings, source_down, coefficients, records,
     send_a, send_b, label_a, label_b,
     got_a, got_b, code_a, code_b, codes, part_a, part_b, sum_a, sum_b, spread,
-    local_sem, halo_send, halo_recv, first_send, first_recv, last_send, last_recv,
+    local_sem, halo_send, halo_recv, first_send, first_recv, last_send, last_recv, entered,
 ):
     wide, narrow = sizes
     last = narrow // 2
@@ -77,10 +77,18 @@
 
     barrier = pltpu.get_barrier_semaphore()
 
-    @pl.loop(1, partners)
-    def _(step):
-        for me, device, _ in groups:
-            pl.semaphore_signal(barrier, inc=1, device_id=device((me + step) % partners), device_id_type=MESH)
+    chip_row = 2 * short
+    along_y = [(w, ((y + i) % last) * 2 + core) for i in range(1, last)]
+    along_z = [(((z + i) % last) * short + x, n) for i in range(1, last)]
+
+    def say(semaphore, device):
+        pl.semaphore_signal(semaphore, inc=1, device_id=device, device_id_type=MESH)
+
+    for i in range(1, chip_row):
+        other = (2 * x + core + i) % chip_row
+        say(barrier, (z * short + other // 2, 2 * y + other % 2))
+    for device in along_y + along_z + [(w, (n + narrow + 2 * core - 1) % narrow)]:
+        say(barrier, device)
 
     loads = [
         pltpu.make_async_copy(source, target, local_sem.at[i])
@@ -111,7 +119,9 @@
             own_basis[:, c * panels : (c + 1) * panels], field[clusters + c], NT, preferred_element_type=F32
         ).astype(BF)
 
-    pl.semaphore_wait(barrier, 2 * (partners - 1))
+    pl.semaphore_wait(barrier, chip_row - 1 + 2 * (last - 1) + 1)
+    for device in along_y + along_z:
+        say(entered, device)
 
     halo = []
     middle = field.at[pl.ds(clusters, clusters)]
@@ -142,6 +152,7 @@
                 products.append(jnp.dot(chosen, coefficients[...], preferred_element_type=F32))
             records[at, pair * 128 : (pair + 1) * 128] = jnp.concatenate(products, 1).astype(BF)
 
+    pl.semaphore_wait(entered, 2 * (last - 1))
     for g, ((partner, row, part), (me, device, streams)) in enumerate(zip(places, groups)):
         (label, code), (send, got) = streams
         position = partner * rows + row
@@ -320,8 +331,9 @@
         + [pltpu.VMEM((partners, 128), F32)]
         + [pltpu.VMEM((last, clusters, half), BF)] * 4
         + [pltpu.VMEM((rank * clusters, columns), F32)]
-        + [dma((4,)), dma((4,)), dma((4,)), dma((4,)), dma((4,)), dma((2,)), dma((2,))],
-        compiler_params=pltpu.CompilerParams(vmem_limit_bytes=48 << 20, has_side_effects=True, collective_id=0),
+        + [dma((4,)), dma((4,)), dma((4,)), dma((4,)), dma((4,)), dma((2,)), dma((2,))]
+        + [pltpu.SemaphoreType.REGULAR],
+        compiler_params=pltpu.CompilerParams(vmem_limit_bytes=56 << 20, has_side_effects=True, collective_id=0),
         cost_estimate=pl.CostEstimate(flops=40_000_000_000, bytes_accessed=6_000_000, transcendentals=12_000_000),
     )(
         near_list.T, excitation, coords, basis, couplings,

time: 71.5 us -> 64.9 us (0.908)
  the two profiles are of different devices: /device:TPU:1 before, /device:TPU:4 now
where the time goes in v3:
time: 64.9 us; the launch traced here: 64.7 us
  Pallas kernels  62.8 us (97%)
  local copies, waits for them, and re-layouts  1.87 us (3%)
    pallas_call x1, Pallas kernels, shards(): pl.pallas_call(functools.partial(main_kernel, (wide, narrow), clusters, e...  62.8 us
    unnamed x1, local copies, waits for them, and re-layouts  1.87 us

profile of v3, /device:TPU:4, one launch (start us, length us, event | category | flops | bytes accessed | tf_op | source)
XLA Modules:
  0.0 64.7 jit_solution(3801161302303770193)
XLA Ops:
  0.0 62.8 %shard_map.82 = bf16[64,4096]{1,0:T(8,128)(2,1)} custom-call(s32[24,32]{1,0:T(8,128)} %bitcast.4, bf16[64,4096]{1,0:T(8,128)(2,1)} %excitation.1, bf16[3,4096]{1,0:T(4,128)(2,1)} %coords.1, bf16[16,4096]{1,0:T(8,128)(2,1)} %basis.1, bf16[512,256]{1,0:T(8,128)(2,1)} %couplings.1, s32[1,512]{1,0:T(1,128)} %bitcast.5, s32[1,512]{1,0:T(1,128)} %bitcast.6, ...), custom_call_target="tpu_custom_call" | custom-call | flops 40000000000 | bytes 6000000 | tf_op jit(solution)/shard_map/pallas_call | solution.py:306
  62.8 1.9 %copy.10 = bf16[64,4096]{1,0:T(8,128)(2,1)} copy(bf16[64,4096]{1,0:T(8,128)(2,1)} %shard_map.82) | data formatting | bytes 1048576

commit v4 on v3

--- a/solution.py
+++ b/solution.py
@@ -9,8 +9,8 @@
 from jax.sharding import PartitionSpec as P
 
 SOFTEN = 0.0025
-FIRST_NEAR = 18
-SECOND_NEAR = 20
+FIRST_NEAR = 23
+SECOND_NEAR = 25
 BF = jnp.bfloat16
 F32 = jnp.float32
 MESH = pl.DeviceIdType.MESH
@@ -57,37 +57,49 @@
     last = narrow // 2
     short = wide // last
     w, n = lax.axis_index("wide"), lax.axis_index("narrow")
-    z, x, y, core = w // short, w % short, n // 2, n % 2
+    z, x, y, core = lax.div(w, short), lax.rem(w, short), lax.div(n, 2), lax.rem(n, 2)
     columns, own = excitation.shape
     panels = own // clusters
     rank = basis.shape[0]
     pairs = couplings.shape[0]
     group = panels // rank
     partners, rows, half = send_a.shape
-    after, before = (n + 1) % narrow, (n + narrow - 1) % narrow
+    after, before = lax.rem(n + 1, narrow), lax.rem(n + narrow - 1, narrow)
     me_a, me_b = x * narrow + n, w * 2 + core
 
-    def device_a(p):
-        return (z * short + p // narrow, p % narrow)
-
-    def device_b(p):
-        return (p // 2, y * 2 + p % 2)
-
-    groups = ((me_a, device_a, ((label_a, code_a), (send_a, got_a))), (me_b, device_b, ((label_b, code_b), (send_b, got_b))))
+    def partners_a(visit):
+        for i in range(short):
+            column = lax.rem(x + i, short)
+
+            @pl.loop(0 if i else 1, narrow, unroll=3 if i == 0 else 4)
+            def _(step):
+                there = lax.rem(n + step, narrow)
+                visit(column * narrow + there, (z * short + column, there))
+
+    def partners_b(visit):
+        for i in range(2):
+            side = lax.rem(core + i, 2)
+
+            @pl.loop(0 if i else 1, wide, unroll=4 if i else 1)
+            def _(step):
+                there = lax.rem(w + step, wide)
+                visit(there * 2 + side, (there, y * 2 + side))
+
+    groups = ((me_a, partners_a, ((label_a, code_a), (send_a, got_a))), (me_b, partners_b, ((label_b, code_b), (send_b, got_b))))
 
     barrier = pltpu.get_barrier_semaphore()
 
     chip_row = 2 * short
-    along_y = [(w, ((y + i) % last) * 2 + core) for i in range(1, last)]
-    along_z = [(((z + i) % last) * short + x, n) for i in range(1, last)]
+    along_y = [(w, lax.rem(y + i, last) * 2 + core) for i in range(1, last)]
+    along_z = [(lax.rem(z + i, last) * short + x, n) for i in range(1, last)]
 
     def say(semaphore, device):
         pl.semaphore_signal(semaphore, inc=1, device_id=device, device_id_type=MESH)
 
     for i in range(1, chip_row):
-        other = (2 * x + core + i) % chip_row
-        say(barrier, (z * short + other // 2, 2 * y + other % 2))
-    for device in along_y + along_z + [(w, (n + narrow + 2 * core - 1) % narrow)]:
+        other = lax.rem(2 * x + core + i, chip_row)
+        say(barrier, (z * short + lax.div(other, 2), 2 * y + lax.rem(other, 2)))
+    for device in along_y + along_z + [(w, lax.rem(n + narrow + 2 * core - 1, narrow))]:
         say(barrier, device)
 
     loads = [
@@ -140,21 +152,19 @@
 
     block = 64
     lane = iota((block, 128), 1)
-    for q in range(0, pairs, block):
-        at = slice(q, q + block)
-        mine = [source_down[at, :] == (lane // rank + g * group).astype(F32) for g in range(clusters // group)]
-        for pair in range(rank // 2):
-            products = []
-            for a in (2 * pair, 2 * pair + 1):
-                across = own_couplings[at, (a // group) * 128 : (a // group + 1) * 128].astype(F32)
-                tiled = jnp.take_along_axis(across, (a % group) * rank + lane % rank, axis=1)
-                chosen = jnp.concatenate([jnp.where(m, tiled, 0.0).astype(BF) for m in mine], 1)
-                products.append(jnp.dot(chosen, coefficients[...], preferred_element_type=F32))
-            records[at, pair * 128 : (pair + 1) * 128] = jnp.concatenate(products, 1).astype(BF)
-
-    pl.semaphore_wait(entered, 2 * (last - 1))
-    for g, ((partner, row, part), (me, device, streams)) in enumerate(zip(places, groups)):
+    for g, ((partner, row, part), (me, visits, streams)) in enumerate(zip(places, groups)):
         (label, code), (send, got) = streams
+        for q in range(0, pairs, block):
+            at = slice(q, q + block)
+            mine = [source_down[at, :] == (lane // rank + i * group).astype(F32) for i in range(clusters // group)]
+            for pair in range(g * rank // 4, (g + 1) * rank // 4):
+                products = []
+                for a in (2 * pair, 2 * pair + 1):
+                    across = own_couplings[at, (a // group) * 128 : (a // group + 1) * 128].astype(F32)
+                    tiled = jnp.take_along_axis(across, (a % group) * rank + lane % rank, axis=1)
+                    chosen = jnp.concatenate([jnp.where(m, tiled, 0.0).astype(BF) for m in mine], 1)
+                    products.append(jnp.dot(chosen, coefficients[...], preferred_element_type=F32))
+                records[at, pair * 128 : (pair + 1) * 128] = jnp.concatenate(products, 1).astype(BF)
         position = partner * rows + row
         for p in range(0, partners, 16):
             choice = onehot(position == iota((16 * rows, pairs), 0) + p * rows)
@@ -166,15 +176,17 @@
         for p in range(partners):
             label[p] = table[p : p + 1]
 
-        @pl.loop(1, partners)
-        def _(step):
-            there = (me + step) % partners
+        def send_to(there, device):
             for i, (source, target) in enumerate(streams):
                 pltpu.make_async_remote_copy(
                     src_ref=source.at[there], dst_ref=target.at[me],
                     send_sem=first_send.at[2 * g + i], recv_sem=first_recv.at[2 * g + i],
-                    device_id=device(there), device_id_type=MESH,
+                    device_id=device, device_id_type=MESH,
                 ).start()
+
+        if g == 0:
+            pl.semaphore_wait(entered, 2 * (last - 1))
+        visits(send_to)
 
         for i, (source, target) in enumerate(streams):
             pltpu.make_async_copy(source.at[me], target.at[me], first_recv.at[2 * g + i]).start()
@@ -237,7 +249,6 @@
     for g, (got, code, part, final) in enumerate(((got_a, code_a, part_a, sum_a), (got_b, code_b, part_b, sum_b))):
         near_clusters(0 if g == 0 else FIRST_NEAR, FIRST_NEAR if g == 0 else SECOND_NEAR)
         pltpu.make_async_copy(code, code, first_recv.at[2 * g]).wait()
-        pltpu.make_async_copy(got, got, first_recv.at[2 * g + 1]).wait()
         for p in range(partners):
             codes[p : p + 1, :] = code[p]
         slots = partners * rows
@@ -248,6 +259,7 @@
         )
         picked = jnp.where(iota((slots, 128), 0) % rows == iota((slots, 128), 1), copied, 0.0).astype(BF)
         along = lax.dot_general(jnp.ones((8, 128), BF), picked, NT, preferred_element_type=F32)[0:1].astype(jnp.int32)
+        pltpu.make_async_copy(got, got, first_recv.at[2 * g + 1]).wait()
         arrived = got[...].reshape(slots, half)
         for p in range(0, last, 2):
             choice = onehot(along == iota((2 * clusters, slots), 0) + (p * clusters + 1))
@@ -257,7 +269,7 @@
 
         @pl.loop(1, last)
         def _(step):
-            there = (me + step) % last
+            there = lax.rem(me + step, last)
             device = (there * short + x, n) if g == 0 else (w, there * 2 + core)
             pltpu.make_async_remote_copy(
                 src_ref=part.at[there], dst_ref=final.at[me], send_sem=last_send.at[g], recv_sem=last_recv.at[g],

time: 64.9 us -> 64.4 us (level)
  the two profiles are of different devices: /device:TPU:4 before, /device:TPU:1 now
where the time goes in v4:
time: 64.4 us; the launch traced here: 64.2 us
  Pallas kernels  62.3 us (97%)
  local copies, waits for them, and re-layouts  1.87 us (3%)
    pallas_call x1, Pallas kernels, shards(): pl.pallas_call(functools.partial(main_kernel, (wide, narrow), clusters, e...  62.3 us
    unnamed x1, local copies, waits for them, and re-layouts  1.87 us

profile of v4, /device:TPU:1, one launch (start us, length us, event | category | flops | bytes accessed | tf_op | source)
XLA Modules:
  0.0 64.2 jit_solution(3333403323044671540)
XLA Ops:
  0.0 62.3 %shard_map.82 = bf16[64,4096]{1,0:T(8,128)(2,1)} custom-call(s32[24,32]{1,0:T(8,128)} %bitcast.4, bf16[64,4096]{1,0:T(8,128)(2,1)} %excitation.1, bf16[3,4096]{1,0:T(4,128)(2,1)} %coords.1, bf16[16,4096]{1,0:T(8,128)(2,1)} %basis.1, bf16[512,256]{1,0:T(8,128)(2,1)} %couplings.1, s32[1,512]{1,0:T(1,128)} %bitcast.5, s32[1,512]{1,0:T(1,128)} %bitcast.6, ...), custom_call_target="tpu_custom_call" | custom-call | flops 40000000000 | bytes 6000000 | tf_op jit(solution)/shard_map/pallas_call | solution.py:318
  62.3 1.9 %copy.10 = bf16[64,4096]{1,0:T(8,128)(2,1)} copy(bf16[64,4096]{1,0:T(8,128)(2,1)} %shard_map.82) | data formatting | bytes 1048576

commit v5 on v4

--- a/solution.py
+++ b/solution.py
@@ -67,13 +67,17 @@
     after, before = lax.rem(n + 1, narrow), lax.rem(n + narrow - 1, narrow)
     me_a, me_b = x * narrow + n, w * 2 + core
 
+    def both_ways(step, count):
+        odd = lax.rem(step, 2)
+        return odd * lax.div(step + 1, 2) + (1 - odd) * (count - lax.div(step, 2))
+
     def partners_a(visit):
         for i in range(short):
             column = lax.rem(x + i, short)
 
             @pl.loop(0 if i else 1, narrow, unroll=3 if i == 0 else 4)
             def _(step):
-                there = lax.rem(n + step, narrow)
+                there = lax.rem(n + both_ways(step, narrow), narrow)
                 visit(column * narrow + there, (z * short + column, there))
 
     def partners_b(visit):
@@ -82,7 +86,7 @@
 
             @pl.loop(0 if i else 1, wide, unroll=4 if i else 1)
             def _(step):
-                there = lax.rem(w + step, wide)
+                there = lax.rem(w + both_ways(step, wide), wide)
                 visit(there * 2 + side, (there, y * 2 + side))
 
     groups = ((me_a, partners_a, ((label_a, code_a), (send_a, got_a))), (me_b, partners_b, ((label_b, code_b), (send_b, got_b))))
@@ -269,7 +273,7 @@
 
         @pl.loop(1, last)
         def _(step):
-            there = lax.rem(me + step, last)
+            there = lax.rem(me + both_ways(step, last), last)
             device = (there * short + x, n) if g == 0 else (w, there * 2 + core)
             pltpu.make_async_remote_copy(
                 src_ref=part.at[there], dst_ref=final.at[me], send_sem=last_send.at[g], recv_sem=last_recv.at[g],

time: 64.4 us -> 64.2 us (level)
  the two profiles are of different devices: /device:TPU:1 before, /device:TPU:67 now
where the time goes in v5:
time: 64.2 us; the launch traced here: 64 us
  Pallas kernels  62.1 us (97%)
  local copies, waits for them, and re-layouts  1.87 us (3%)
    pallas_call x1, Pallas kernels, shards(): pl.pallas_call(functools.partial(main_kernel, (wide, narrow), clusters, e...  62.1 us
    unnamed x1, local copies, waits for them, and re-layouts  1.87 us

profile of v5, /device:TPU:67, one launch (start us, length us, event | category | flops | bytes accessed | tf_op | source)
XLA Modules:
  0.0 64.0 jit_solution(4862987201755173982)
XLA Ops:
  0.0 62.1 %shard_map.82 = bf16[64,4096]{1,0:T(8,128)(2,1)} custom-call(s32[24,32]{1,0:T(8,128)} %bitcast.4, bf16[64,4096]{1,0:T(8,128)(2,1)} %excitation.1, bf16[3,4096]{1,0:T(4,128)(2,1)} %coords.1, bf16[16,4096]{1,0:T(8,128)(2,1)} %basis.1, bf16[512,256]{1,0:T(8,128)(2,1)} %couplings.1, s32[1,512]{1,0:T(1,128)} %bitcast.5, s32[1,512]{1,0:T(1,128)} %bitcast.6, ...), custom_call_target="tpu_custom_call" | custom-call | flops 40000000000 | bytes 6000000 | tf_op jit(solution)/shard_map/pallas_call | solution.py:322
  62.1 1.9 %copy.10 = bf16[64,4096]{1,0:T(8,128)(2,1)} copy(bf16[64,4096]{1,0:T(8,128)(2,1)} %shard_map.82) | data formatting | bytes 1048576

commit v6 on v4

--- a/solution.py
+++ b/solution.py
@@ -9,8 +9,8 @@
 from jax.sharding import PartitionSpec as P
 
 SOFTEN = 0.0025
-FIRST_NEAR = 23
-SECOND_NEAR = 25
+FIRST_NEAR = 22
+SECOND_NEAR = 22
 BF = jnp.bfloat16
 F32 = jnp.float32
 MESH = pl.DeviceIdType.MESH

time: 64.4 us -> 62.8 us (0.975)
  Pallas kernels: 62.3 us -> 60.7 us
    pallas_call x1, Pallas kernels: 62.3 us -> 60.7 us  [shards(): pl.pallas_call(functools.partial(main_kernel, (wide, narrow), clusters, e...]
where the time goes in v6:
time: 62.8 us; the launch traced here: 62.5 us
  Pallas kernels  60.7 us (97%)
  local copies, waits for them, and re-layouts  1.87 us (3%)
    pallas_call x1, Pallas kernels, shards(): pl.pallas_call(functools.partial(main_kernel, (wide, narrow), clusters, e...  60.7 us
    unnamed x1, local copies, waits for them, and re-layouts  1.87 us

profile of v6, /device:TPU:1, one launch (start us, length us, event | category | flops | bytes accessed | tf_op | source)
XLA Modules:
  0.0 62.5 jit_solution(12978708318669186905)
XLA Ops:
  0.0 60.7 %shard_map.82 = bf16[64,4096]{1,0:T(8,128)(2,1)} custom-call(s32[24,32]{1,0:T(8,128)} %bitcast.4, bf16[64,4096]{1,0:T(8,128)(2,1)} %excitation.1, bf16[3,4096]{1,0:T(4,128)(2,1)} %coords.1, bf16[16,4096]{1,0:T(8,128)(2,1)} %basis.1, bf16[512,256]{1,0:T(8,128)(2,1)} %couplings.1, s32[1,512]{1,0:T(1,128)} %bitcast.5, s32[1,512]{1,0:T(1,128)} %bitcast.6, ...), custom_call_target="tpu_custom_call" | custom-call | flops 40000000000 | bytes 6000000 | tf_op jit(solution)/shard_map/pallas_call | solution.py:318
  60.7 1.9 %copy.10 = bf16[64,4096]{1,0:T(8,128)(2,1)} copy(bf16[64,4096]{1,0:T(8,128)(2,1)} %shard_map.82) | data formatting | bytes 1048576
